TPU v7x, 32 devices: a whole 2x2x4 slice. The times are simulated.
32 devices in a mesh: view: 8 (over z, x), slab: 4 (over y, core).
Axes of the slice: x: 2, y: 2, z: 4, core: 2. Of those that a mesh axis runs over, the one named last changes fastest.
Arguments:
- volume: float32 [4, 128, 128], P('slab', 'view'), may hold values from 0 to 2
- tile_blocks: bfloat16 [8, 4, 192, 128, 128], P('view', 'slab'), may hold values from 0.0009994507 to 0.014953613
- pixel_tile: int32 [8, 4, 192], P('view', 'slab'), may hold values from 0 to 127, as said below
- ray_tile: int32 [8, 4, 192], P('view', 'slab'), may hold values from 0 to 127, as said below
- counts: int32 [8, 4], P('view', 'slab'), may hold values from 16 to 192, as said below
- subset_views: int32 [8, 4], P('view'), may hold values from 0 to 7, as said below
- sinogram: float32 [8, 128, 128], P('view', 'slab'), may hold values from 0 to 3
- weights: float32 [8, 128, 128], P('view', 'slab'), may hold values from 0.1 to 1
Outputs:
- updated: float32 [4, 128, 128], P('slab', 'view')
- denominators: float32 [4, 128, 128], P('slab', 'view')
Inputs may be any that keep to these rules, and one draw needn't show every extreme that they name: `counts`: for every group exactly one slab has 192 live slots; every count is at least 16. `pixel_tile`: slots k < 16 of group g name volume tiles g * 16 + k in every slab; slots at or past the count hold indices in range and are unused. `ray_tile`: slots at or past the count hold indices in range and are unused. `subset_views`: each group lists 4 distinct views in rising order.
All inputs are finite; a program needn't handle non-finite values.
Results may differ from a plain program's by a relative error of at most 0.00032.
Values may be sent and summed in bfloat16 or wider, within the bound.
No kernel may reach another device: no remote copies, remote signals or barrier semaphores. Data moves between devices by JAX's collectives and lax.ppermute only.
A program may use at most 64 MiB of HBM per device.

v0:
```python
import jax
import jax.numpy as jnp
from jax import lax
from jax.sharding import PartitionSpec as P

VG = 8
SUBSETS = 2


def make_ratio(totals, measured, weight, subset):
    ray_rows = jnp.arange(totals.shape[0], dtype=jnp.int32)
    view_of = ray_rows % VG
    in_subset = jnp.any(subset[None, :] == view_of[:, None], axis=1).astype(jnp.float32)
    denominator_rays = weight * totals[:, 1]
    residual_rays = in_subset[:, None] * weight * (measured - totals[:, 0])
    return jnp.stack([denominator_rays, residual_rays], axis=1).astype(jnp.bfloat16)


def on_device(volume, tile_blocks, pixel_tile, ray_tile, counts, subset_views, sinogram, weights):
    local_tiles = tile_blocks[0, 0]
    pixel_rows = pixel_tile[0, 0]
    ray_rows = ray_tile[0, 0]
    count_here = counts[0, 0]
    subset = subset_views[0]
    ray_total = sinogram.shape[1] * lax.axis_size("slab")
    voxel_total = volume.shape[1] * lax.axis_size("view")
    live_mask = (jnp.arange(local_tiles.shape[0], dtype=jnp.int32) < count_here).astype(jnp.float32)
    own_image = volume[0].astype(jnp.bfloat16)
    slab_image = lax.all_gather(own_image, "view", axis=0, tiled=True)
    picked = slab_image[pixel_rows]
    operand = jnp.stack([picked, jnp.ones_like(picked)], axis=1)
    products = jnp.einsum("krv,kcv->kcr", local_tiles, operand, preferred_element_type=jnp.float32)
    products = products * live_mask[:, None, None]
    partial_rays = jax.ops.segment_sum(products, ray_rows, num_segments=ray_total)
    measured, weight = (
        lax.all_gather(sinogram[0], "slab", axis=0, tiled=True),
        lax.all_gather(weights[0], "slab", axis=0, tiled=True),
    )
    totals = lax.psum(partial_rays, "slab")
    back_in = make_ratio(totals, measured, weight, subset)
    gathered = back_in[ray_rows]
    back_products = jnp.einsum(
        "krv,kcr->kcv", local_tiles, gathered, preferred_element_type=jnp.float32
    )
    back_products = back_products * live_mask[:, None, None]
    partial_voxels = jax.ops.segment_sum(back_products, pixel_rows, num_segments=voxel_total)
    voxel_share = lax.psum_scatter(partial_voxels, "view", scatter_dimension=0, tiled=True)
    denominators = voxel_share[:, 0, :]
    gradient = voxel_share[:, 1, :]
    updated = jnp.maximum(volume[0] + SUBSETS * gradient / denominators, 0.0)
    return (updated[None], denominators[None])


def solution(mesh):
    return jax.shard_map(
        on_device,
        mesh=mesh,
        in_specs=(
            P("slab", "view", None),
            P("view", "slab", None, None, None),
            P("view", "slab", None),
            P("view", "slab", None),
            P("view", "slab"),
            P("view", None),
            P("view", "slab", None),
            P("view", "slab", None),
        ),
        out_specs=(P("slab", "view", None), P("slab", "view", None)),
        check_vma=False,
    )
```

profile of v0, /device:TPU:0, one launch (start us, length us, event | category | flops | bytes accessed | tf_op | source)
XLA Modules:
  0.0 182.9 jit_solution(6079675270705240020)
XLA Ops:
  7.9 0.7 convert_element_type.21
  8.6 32.4 %all-gather.1 = bf16[1,128,128]{2,1,0:T(8,128)(2,1)S(1)} all-gather(bf16[1,16,128]{2,1,0:T(8,128)(2,1)S(1)} %convert_element_type.21), channel_id=3, replica_groups=mesh['view'=8,'slab'=4] {'view'}, dimensions={1}, use_global_device_ids=true | all-gather | bytes 36864 | tf_op jit(solution)/shard_map/all_gather | solution.py:29
  41.0 0.7 compare_select_fusion.1
  41.7 0.8 gather_fusion
  42.5 0.1 copy.19
  42.6 6.1 %fusion.4 = f32[192,2,128]{2,1,0:T(2,128)S(1)} fusion(bf16[1,1,192,128,128]{4,3,2,1,0:T(8,128)(2,1)} %param.9, f32[192]{0:T(256)S(1)} %compare_convert_fusion, bf16[192,1,128]{2,1,0:T(2,128)(2,1)S(1)} %copy.19), kind=kOutput, calls=%fused_computation.8 | convolution fusion | flops 12632064 | bytes 6537984 | tf_op jit(solution)/shard_map/krv,kcv->kcr/dot_general | solution.py:32
  48.8 7.2 %scatter_fusion = f32[128,2,128]{2,1,0:T(2,128)S(1)} fusion(f32[128,2,128]{2,1,0:T(2,128)S(1)} %broadcast.74.clone, s32[192]{0:T(256)S(1)} %bitcast.68, f32[192,2,128]{2,1,0:T(2,128)S(1)} %fusion.4), kind=kCustom, calls=%fused_computation.2 | custom fusion | flops 49152 | bytes 590592 | tf_op jit(solution)/shard_map/scatter-add | solution.py:34
  56.0 0.6 copy-done.1
  56.6 0.0 all-reduce.7.cloned.1.call-start
  56.7 0.1 compare_reduce_fusion
  56.8 5.2 %all-gather = f32[1,128,128]{2,1,0:T(8,128)S(1)} all-gather(f32[1,32,128]{2,1,0:T(8,128)S(1)} %copy-done.4), channel_id=2, replica_groups=mesh['view'=8,'slab'=4] {'slab'}, dimensions={1}, use_global_device_ids=true | all-gather | bytes 81920 | tf_op jit(solution)/shard_map/all_gather | solution.py:37
  62.1 5.2 %all-gather.2 = f32[1,128,128]{2,1,0:T(8,128)S(1)} all-gather(f32[1,32,128]{2,1,0:T(8,128)S(1)} %copy-done.5), channel_id=4, replica_groups=mesh['view'=8,'slab'=4] {'slab'}, dimensions={1}, use_global_device_ids=true | all-gather | bytes 81920 | tf_op jit(solution)/shard_map/all_gather | solution.py:36
  67.3 22.2 %all-reduce.5.cloned.1.call-done = f32[128,2,128]{2,1,0:T(2,128)} async-done(((f32[128,2,128]{2,1,0:T(2,128)}), f32[128,2,128]{2,1,0:T(2,128)}) %all-reduce.5.cloned.1.call-update) | async-done | bytes 131088 | tf_op jit(solution)/shard_map/psum | solution.py:39
  89.5 1.1 fusion.19
  90.5 0.1 fusion.14
  90.7 0.1 copy.21
  90.7 0.8 gather_fusion.1
  91.6 4.5 %fusion.7 = f32[192,2,128]{2,1,0:T(2,128)S(1)} fusion(bf16[192,2,128]{2,1,0:T(2,128)(2,1)S(1)} %gather_fusion.1, bf16[1,1,192,128,128]{4,3,2,1,0:T(8,128)(2,1)} %param.9, f32[192]{0:T(256)S(1)} %compare_convert_fusion), kind=kOutput, calls=%fused_computation.9 | convolution fusion | flops 12632064 | bytes 6587136 | tf_op jit(solution)/shard_map/krv,kcr->kcv/dot_general | solution.py:42
  96.2 7.1 %scatter_fusion.1 = f32[128,2,128]{2,1,0:T(2,128)S(1)} fusion(f32[128,2,128]{2,1,0:T(2,128)S(1)} %broadcast.74, s32[192]{0:T(256)S(1)} %bitcast.69, f32[192,2,128]{2,1,0:T(2,128)S(1)} %fusion.7), kind=kCustom, calls=%fused_computation.3 | custom fusion | flops 49152 | bytes 590592 | tf_op jit(solution)/shard_map/scatter-add | solution.py:46
  103.3 0.6 copy-done
  104.0 0.6 dynamic-slice
  105.2 69.4 %all-reduce.7.cloned.1.call-done = f32[128,2,128]{2,1,0:T(2,128)} async-done(((f32[128,2,128]{2,1,0:T(2,128)}), f32[128,2,128]{2,1,0:T(2,128)}) %all-reduce.7.cloned.1.call-update) | async-done | bytes 131088
  174.6 0.8 constant_dynamic-slice_fusion
  175.5 0.6 fusion.17
  (30 shorter events, 0.2 us)
Async XLA Ops:
  7.2 41.6 %copy-start.6 = (s32[1,1,192]{2,1,0:T(1,128)S(1)}, s32[1,1,192]{2,1,0:T(1,128)}, u32[]{:S(2)}) copy-start(s32[1,1,192]{2,1,0:T(1,128)} %param.11) | copy-start | bytes 2308
  7.2 49.5 %copy-start.8 = (s32[1,4]{1,0:T(1,128)S(1)}, s32[1,4]{1,0:T(1,128)}, u32[]{:S(2)}) copy-start(s32[1,4]{1,0:T(1,128)} %param.13) | copy-start | bytes 52
  7.2 49.6 %copy-start.4 = (f32[1,32,128]{2,1,0:T(8,128)S(1)}, f32[1,32,128]{2,1,0:T(8,128)}, u32[]{:S(2)}) copy-start(f32[1,32,128]{2,1,0:T(8,128)} %param.15) | copy-start | bytes 49156
  7.2 54.9 %copy-start.5 = (f32[1,32,128]{2,1,0:T(8,128)S(1)}, f32[1,32,128]{2,1,0:T(8,128)}, u32[]{:S(2)}) copy-start(f32[1,32,128]{2,1,0:T(8,128)} %param.14) | copy-start | bytes 49156
  7.2 82.2 %all-reduce.5.cloned.1.call-start = ((), (), s32[]{:S(2)}) async-start(), calls=%async_computation | async-start | bytes 262144 | tf_op jit(solution)/shard_map/psum | solution.py:39
  42.6 53.6 %copy-start.7 = (s32[1,1,192]{2,1,0:T(1,128)S(1)}, s32[1,1,192]{2,1,0:T(1,128)}, u32[]{:S(2)}) copy-start(s32[1,1,192]{2,1,0:T(1,128)} %param.10) | copy-start | bytes 2308
  48.7 55.3 %copy-start.9 = (u32[32]{0:T(128)S(1)}, u32[32]{0:T(128)}, u32[]{:S(2)}) copy-start(u32[32]{0:T(128)} %constant.40) | copy-start | bytes 388
  48.7 126.7 %copy-start.2 = (f32[1,16,128]{2,1,0:T(8,128)S(1)}, f32[1,16,128]{2,1,0:T(8,128)}, u32[]{:S(2)}) copy-start(f32[1,16,128]{2,1,0:T(8,128)} %param.8) | copy-start | bytes 24580
  55.9 0.7 copy-start.1
  56.6 118.0 %all-reduce.7.cloned.1.call-start = ((), (), s32[]{:S(2)}) async-start(), calls=%async_computation.1 | async-start | bytes 262144
  103.3 0.7 copy-start
  175.4 0.6 copy-start.3
Sparse Core Ops, SparseCore 0:
  56.7 32.6 all-reduce.4
  104.1 70.4 all-reduce.6
where the time goes:
time: 183 us
  waiting for transfers between devices  91.6 us (50%)
  blocking collectives  42.9 us (23%)
  other arithmetic  16.5 us (9%)
  between operations  15.5 us (8%)
  matrix products  10.7 us (6%)
  local copies, waits for them, and re-layouts  5.65 us (3%)
    unnamed x3, waiting for transfers between devices  69.4 us
    all_gather x1, blocking collectives, on_device(): slab_image = lax.all_gather(own_image, 'view', axis=0, tiled=True)  32.4 us
    psum x1, waiting for transfers between devices, on_device(): totals = lax.psum(partial_rays, 'slab')  22.2 us
    scatter-add x1, other arithmetic, on_device(): jax.ops.segment_sum(products, ray_rows, num_segments=ray_total)  7.15 us
    scatter-add x1, other arithmetic, on_device(): jax.ops.segment_sum(back_products, pixel_rows, num_segments=voxel_total)  7.15 us
    dot_general x1, matrix products, on_device(): jnp.einsum('krv,kcv->kcr', local_tiles, operand, preferred_element_type=j...  6.14 us
    all_gather x1, blocking collectives, on_device(): lax.all_gather(sinogram[0], 'slab', axis=0, tiled=True)  5.24 us
    all_gather x1, blocking collectives, on_device(): lax.all_gather(weights[0], 'slab', axis=0, tiled=True)  5.24 us
  transfers between devices with their start and end apart: 2, of which 2 were waited for; matrix products, arithmetic and copies ran while one was open for 0% of the time, Pallas kernels for 0%

commit v1 on v0

--- a/solution.py
+++ b/solution.py
@@ -5,6 +5,19 @@
 
 VG = 8
 SUBSETS = 2
+
+
+def assign_notes(which_axis, s0):
+    chips = lax.axis_size(which_axis)
+    moved = [None] * chips
+    moved[chips - 1] = s0
+    in_order = tuple(((m, (m + 1) % chips) for m in range(chips)))
+    for b in range(chips - 2, -1, -1):
+        moved[b] = lax.ppermute(moved[b + 1], axis_name=which_axis, perm=in_order)
+    v1 = jnp.concatenate(moved, 0)
+    x_new = (lax.axis_index(which_axis) + 1) * s0.shape[0]
+    t1 = jnp.roll(v1, x_new, 0)
+    return t1
 
 
 def make_ratio(totals, measured, weight, subset):
@@ -26,7 +39,7 @@
     voxel_total = volume.shape[1] * lax.axis_size("view")
     live_mask = (jnp.arange(local_tiles.shape[0], dtype=jnp.int32) < count_here).astype(jnp.float32)
     own_image = volume[0].astype(jnp.bfloat16)
-    slab_image = lax.all_gather(own_image, "view", axis=0, tiled=True)
+    slab_image = assign_notes("view", own_image)
     picked = slab_image[pixel_rows]
     operand = jnp.stack([picked, jnp.ones_like(picked)], axis=1)
     products = jnp.einsum("krv,kcv->kcr", local_tiles, operand, preferred_element_type=jnp.float32)

time: 183 us -> 193 us (1.055)
  waiting for transfers between devices: 91.6 us -> 129 us
  blocking collectives: 42.9 us -> 10.5 us
  starting transfers between devices: 0.08 us -> 3.06 us
  other arithmetic: 16.5 us -> 18.6 us
    ppermute x0 -> x7, waiting for transfers between devices: none -> 40.4 us  [assign_notes(): moved[b] = lax.ppermute(moved[b + 1], axis_name=which_axis, perm=in_order)]
    all_gather x1 -> x0, blocking collectives: 32.4 us -> none  [on_device(): slab_image = lax.all_gather(own_image, 'view', axis=0, tiled=True)]
    psum x1, waiting for transfers between devices: 22.2 us -> 18.8 us  [on_device(): totals = lax.psum(partial_rays, 'slab')]
    ppermute x0 -> x7, starting transfers between devices: none -> 2.98 us  [assign_notes(): moved[b] = lax.ppermute(moved[b + 1], axis_name=which_axis, perm=in_order)]
  transfers between devices with their start and end apart: 2 -> 9, of which waited for: 2 -> 9; matrix products, arithmetic and copies ran while one was open for 0% -> 1% of each run, Pallas kernels for 0% -> 0%
where the time goes in v1:
time: 193 us
  waiting for transfers between devices  129 us (67%)
  other arithmetic  18.6 us (10%)
  between operations  15.5 us (8%)
  matrix products  10.7 us (6%)
  blocking collectives  10.5 us (5%)
  local copies, waits for them, and re-layouts  5.75 us (3%)
  starting transfers between devices  3.06 us (2%)
    unnamed x3, waiting for transfers between devices  69.4 us
    ppermute x7, waiting for transfers between devices, assign_notes(): moved[b] = lax.ppermute(moved[b + 1], axis_name=which_axis, perm=in_order)  40.4 us
    psum x1, waiting for transfers between devices, on_device(): totals = lax.psum(partial_rays, 'slab')  18.8 us
    scatter-add x1, other arithmetic, on_device(): jax.ops.segment_sum(products, ray_rows, num_segments=ray_total)  7.15 us
    scatter-add x1, other arithmetic, on_device(): jax.ops.segment_sum(back_products, pixel_rows, num_segments=voxel_total)  7.15 us
    dot_general x1, matrix products, on_device(): jnp.einsum('krv,kcv->kcr', local_tiles, operand, preferred_element_type=j...  6.14 us
    all_gather x1, blocking collectives, on_device(): lax.all_gather(weights[0], 'slab', axis=0, tiled=True)  5.23 us
    all_gather x1, blocking collectives, on_device(): lax.all_gather(sinogram[0], 'slab', axis=0, tiled=True)  5.23 us
  transfers between devices with their start and end apart: 9, of which 9 were waited for; matrix products, arithmetic and copies ran while one was open for 1% of the time, Pallas kernels for 0%

profile of v1, /device:TPU:0, one launch (start us, length us, event | category | flops | bytes accessed | tf_op | source)
XLA Modules:
  0.0 192.7 jit_solution(15526632408230778195)
XLA Ops:
  7.3 0.7 convert_bitcast_fusion
  8.0 3.0 %collective-permute-start = (bf16[16,128]{1,0:T(8,128)(2,1)S(1)}, bf16[16,128]{1,0:T(8,128)(2,1)S(1)}, u32[]{:S(2)}, u32[]{:S(2)}) collective-permute-start(bf16[16,128]{1,0:T(8,128)(2,1)S(1)} %convert_bitcast_fusion), channel_id=1, source_target_pairs={{0,4},{4,8},{8,12},{12,16},{16,20},{20,24},{24,28},{28,0},{1,5},{5... | collective-permute-start | bytes 12296 | tf_op jit(solution)/shard_map/ppermute | solution.py:16
  10.9 4.6 %collective-permute-done = bf16[16,128]{1,0:T(8,128)(2,1)S(1)} collective-permute-done((bf16[16,128]{1,0:T(8,128)(2,1)S(1)}, bf16[16,128]{1,0:T(8,128)(2,1)S(1)}, u32[]{:S(2)}, u32[]{:S(2)}) %collective-permute-start) | collective-permute-done | bytes 4128 | tf_op jit(solution)/shard_map/ppermute | solution.py:16
  15.5 6.3 %collective-permute-done.1 = bf16[16,128]{1,0:T(8,128)(2,1)S(1)} collective-permute-done((bf16[16,128]{1,0:T(8,128)(2,1)S(1)}, bf16[16,128]{1,0:T(8,128)(2,1)S(1)}, u32[]{:S(2)}, u32[]{:S(2)}) %collective-permute-start.1) | collective-permute-done | bytes 4128 | tf_op jit(solution)/shard_map/ppermute | solution.py:16
  21.9 0.7 compare_select_fusion
  22.5 5.6 %collective-permute-done.2 = bf16[16,128]{1,0:T(8,128)(2,1)S(1)} collective-permute-done((bf16[16,128]{1,0:T(8,128)(2,1)S(1)}, bf16[16,128]{1,0:T(8,128)(2,1)S(1)}, u32[]{:S(2)}, u32[]{:S(2)}) %collective-permute-start.2) | collective-permute-done | bytes 4128 | tf_op jit(solution)/shard_map/ppermute | solution.py:16
  28.8 5.6 %collective-permute-done.3 = bf16[16,128]{1,0:T(8,128)(2,1)S(1)} collective-permute-done((bf16[16,128]{1,0:T(8,128)(2,1)S(1)}, bf16[16,128]{1,0:T(8,128)(2,1)S(1)}, u32[]{:S(2)}, u32[]{:S(2)}) %collective-permute-start.3) | collective-permute-done | bytes 4128 | tf_op jit(solution)/shard_map/ppermute | solution.py:16
  35.1 5.6 %collective-permute-done.4 = bf16[16,128]{1,0:T(8,128)(2,1)S(1)} collective-permute-done((bf16[16,128]{1,0:T(8,128)(2,1)S(1)}, bf16[16,128]{1,0:T(8,128)(2,1)S(1)}, u32[]{:S(2)}, u32[]{:S(2)}) %collective-permute-start.4) | collective-permute-done | bytes 4128 | tf_op jit(solution)/shard_map/ppermute | solution.py:16
  40.8 6.3 %collective-permute-done.5 = bf16[16,128]{1,0:T(8,128)(2,1)S(1)} collective-permute-done((bf16[16,128]{1,0:T(8,128)(2,1)S(1)}, bf16[16,128]{1,0:T(8,128)(2,1)S(1)}, u32[]{:S(2)}, u32[]{:S(2)}) %collective-permute-start.5) | collective-permute-done | bytes 4128 | tf_op jit(solution)/shard_map/ppermute | solution.py:16
  47.1 6.3 %collective-permute-done.6 = bf16[16,128]{1,0:T(8,128)(2,1)S(1)} collective-permute-done((bf16[16,128]{1,0:T(8,128)(2,1)S(1)}, bf16[16,128]{1,0:T(8,128)(2,1)S(1)}, u32[]{:S(2)}, u32[]{:S(2)}) %collective-permute-start.6) | collective-permute-done | bytes 4128 | tf_op jit(solution)/shard_map/ppermute | solution.py:16
  53.4 0.7 constant_dynamic-update-slice_fusion.8
  54.2 0.7 constant_dynamic-update-slice_fusion
  54.9 0.8 gather_fusion
  55.8 6.1 %fusion.4 = f32[192,2,128]{2,1,0:T(2,128)S(1)} fusion(bf16[1,1,192,128,128]{4,3,2,1,0:T(8,128)(2,1)} %param.9, f32[192]{0:T(256)S(1)} %compare_convert_fusion, bf16[192,1,128]{2,1,0:T(2,128)(2,1)S(1)} %copy.19), kind=kOutput, calls=%fused_computation.8 | convolution fusion | flops 12632064 | bytes 6537984 | tf_op jit(solution)/shard_map/krv,kcv->kcr/dot_general | solution.py:45
  62.0 7.2 %scatter_fusion = f32[128,2,128]{2,1,0:T(2,128)S(1)} fusion(f32[128,2,128]{2,1,0:T(2,128)S(1)} %broadcast.75.clone, s32[192]{0:T(256)S(1)} %bitcast.72, f32[192,2,128]{2,1,0:T(2,128)S(1)} %fusion.4), kind=kCustom, calls=%fused_computation.2 | custom fusion | flops 49152 | bytes 590592 | tf_op jit(solution)/shard_map/scatter-add | solution.py:47
  70.0 5.2 %all-gather = f32[1,128,128]{2,1,0:T(8,128)S(1)} all-gather(f32[1,32,128]{2,1,0:T(8,128)S(1)} %copy-done.4), channel_id=2, replica_groups=mesh['view'=8,'slab'=4] {'slab'}, dimensions={1}, use_global_device_ids=true | all-gather | bytes 81920 | tf_op jit(solution)/shard_map/all_gather | solution.py:50
  75.2 5.2 %all-gather.1 = f32[1,128,128]{2,1,0:T(8,128)S(1)} all-gather(f32[1,32,128]{2,1,0:T(8,128)S(1)} %copy-done.5), channel_id=3, replica_groups=mesh['view'=8,'slab'=4] {'slab'}, dimensions={1}, use_global_device_ids=true | all-gather | bytes 81920 | tf_op jit(solution)/shard_map/all_gather | solution.py:49
  80.4 18.8 %all-reduce.5.cloned.1.call-done = f32[128,2,128]{2,1,0:T(2,128)} async-done(((f32[128,2,128]{2,1,0:T(2,128)}), f32[128,2,128]{2,1,0:T(2,128)}) %all-reduce.5.cloned.1.call-update) | async-done | bytes 131088 | tf_op jit(solution)/shard_map/psum | solution.py:52
  99.2 1.1 fusion.19
  100.5 0.8 gather_fusion.1
  101.3 4.5 %fusion.7 = f32[192,2,128]{2,1,0:T(2,128)S(1)} fusion(bf16[192,2,128]{2,1,0:T(2,128)(2,1)S(1)} %gather_fusion.1, bf16[1,1,192,128,128]{4,3,2,1,0:T(8,128)(2,1)} %param.9, f32[192]{0:T(256)S(1)} %compare_convert_fusion), kind=kOutput, calls=%fused_computation.9 | convolution fusion | flops 12632064 | bytes 6587136 | tf_op jit(solution)/shard_map/krv,kcr->kcv/dot_general | solution.py:55
  105.9 7.1 %scatter_fusion.1 = f32[128,2,128]{2,1,0:T(2,128)S(1)} fusion(f32[128,2,128]{2,1,0:T(2,128)S(1)} %broadcast.75, s32[192]{0:T(256)S(1)} %bitcast.73, f32[192,2,128]{2,1,0:T(2,128)S(1)} %fusion.7), kind=kCustom, calls=%fused_computation.3 | custom fusion | flops 49152 | bytes 590592 | tf_op jit(solution)/shard_map/scatter-add | solution.py:59
  115.0 69.4 %all-reduce.7.cloned.1.call-done = f32[128,2,128]{2,1,0:T(2,128)} async-done(((f32[128,2,128]{2,1,0:T(2,128)}), f32[128,2,128]{2,1,0:T(2,128)}) %all-reduce.7.cloned.1.call-update) | async-done | bytes 131088
  184.4 0.8 constant_dynamic-slice_fusion
  (59 shorter events, 3.9 us)
Async XLA Ops:
  7.2 54.8 %copy-start.6 = (s32[1,1,192]{2,1,0:T(1,128)S(1)}, s32[1,1,192]{2,1,0:T(1,128)}, u32[]{:S(2)}) copy-start(s32[1,1,192]{2,1,0:T(1,128)} %param.11) | copy-start | bytes 2308
  7.2 62.7 %copy-start.8 = (s32[1,4]{1,0:T(1,128)S(1)}, s32[1,4]{1,0:T(1,128)}, u32[]{:S(2)}) copy-start(s32[1,4]{1,0:T(1,128)} %param.13) | copy-start | bytes 52
  7.2 62.8 %copy-start.4 = (f32[1,32,128]{2,1,0:T(8,128)S(1)}, f32[1,32,128]{2,1,0:T(8,128)}, u32[]{:S(2)}) copy-start(f32[1,32,128]{2,1,0:T(8,128)} %param.15) | copy-start | bytes 49156
  7.2 68.0 %copy-start.5 = (f32[1,32,128]{2,1,0:T(8,128)S(1)}, f32[1,32,128]{2,1,0:T(8,128)}, u32[]{:S(2)}) copy-start(f32[1,32,128]{2,1,0:T(8,128)} %param.14) | copy-start | bytes 49156
  7.2 92.0 %all-reduce.5.cloned.1.call-start = ((), (), s32[]{:S(2)}) async-start(), calls=%async_computation | async-start | bytes 262144 | tf_op jit(solution)/shard_map/psum | solution.py:52
  8.0 7.6 %collective-permute-start = (bf16[16,128]{1,0:T(8,128)(2,1)S(1)}, bf16[16,128]{1,0:T(8,128)(2,1)S(1)}, u32[]{:S(2)}, u32[]{:S(2)}) collective-permute-start(bf16[16,128]{1,0:T(8,128)(2,1)S(1)} %convert_bitcast_fusion), channel_id=1, source_target_pairs={{0,4},{4,8},{8,12},{12,16},{16,20},{20,24},{24,28},{28,0},{1,5},{5... | collective-permute-start | bytes 12296 | tf_op jit(solution)/shard_map/ppermute | solution.py:16
  15.5 6.3 %collective-permute-start.1 = (bf16[16,128]{1,0:T(8,128)(2,1)S(1)}, bf16[16,128]{1,0:T(8,128)(2,1)S(1)}, u32[]{:S(2)}, u32[]{:S(2)}) collective-permute-start(bf16[16,128]{1,0:T(8,128)(2,1)S(1)} %collective-permute-done), channel_id=1, source_target_pairs={{0,4},{4,8},{8,12},{12,16},{16,20},{20,24},{24,28},{28,0},{1,5},{5... | collective-permute-start | bytes 12296 | tf_op jit(solution)/shard_map/ppermute | solution.py:16
  21.8 6.3 %collective-permute-start.2 = (bf16[16,128]{1,0:T(8,128)(2,1)S(1)}, bf16[16,128]{1,0:T(8,128)(2,1)S(1)}, u32[]{:S(2)}, u32[]{:S(2)}) collective-permute-start(bf16[16,128]{1,0:T(8,128)(2,1)S(1)} %collective-permute-done.1), channel_id=1, source_target_pairs={{0,4},{4,8},{8,12},{12,16},{16,20},{20,24},{24,28},{28,0},{1,5},{5... | collective-permute-start | bytes 12296 | tf_op jit(solution)/shard_map/ppermute | solution.py:16
  28.2 6.3 %collective-permute-start.3 = (bf16[16,128]{1,0:T(8,128)(2,1)S(1)}, bf16[16,128]{1,0:T(8,128)(2,1)S(1)}, u32[]{:S(2)}, u32[]{:S(2)}) collective-permute-start(bf16[16,128]{1,0:T(8,128)(2,1)S(1)} %collective-permute-done.2), channel_id=1, source_target_pairs={{0,4},{4,8},{8,12},{12,16},{16,20},{20,24},{24,28},{28,0},{1,5},{5... | collective-permute-start | bytes 12296 | tf_op jit(solution)/shard_map/ppermute | solution.py:16
  34.5 6.3 %collective-permute-start.4 = (bf16[16,128]{1,0:T(8,128)(2,1)S(1)}, bf16[16,128]{1,0:T(8,128)(2,1)S(1)}, u32[]{:S(2)}, u32[]{:S(2)}) collective-permute-start(bf16[16,128]{1,0:T(8,128)(2,1)S(1)} %collective-permute-done.3), channel_id=1, source_target_pairs={{0,4},{4,8},{8,12},{12,16},{16,20},{20,24},{24,28},{28,0},{1,5},{5... | collective-permute-start | bytes 12296 | tf_op jit(solution)/shard_map/ppermute | solution.py:16
  40.8 6.3 %collective-permute-start.5 = (bf16[16,128]{1,0:T(8,128)(2,1)S(1)}, bf16[16,128]{1,0:T(8,128)(2,1)S(1)}, u32[]{:S(2)}, u32[]{:S(2)}) collective-permute-start(bf16[16,128]{1,0:T(8,128)(2,1)S(1)} %collective-permute-done.4), channel_id=1, source_target_pairs={{0,4},{4,8},{8,12},{12,16},{16,20},{20,24},{24,28},{28,0},{1,5},{5... | collective-permute-start | bytes 12296 | tf_op jit(solution)/shard_map/ppermute | solution.py:16
  47.1 6.3 %collective-permute-start.6 = (bf16[16,128]{1,0:T(8,128)(2,1)S(1)}, bf16[16,128]{1,0:T(8,128)(2,1)S(1)}, u32[]{:S(2)}, u32[]{:S(2)}) collective-permute-start(bf16[16,128]{1,0:T(8,128)(2,1)S(1)} %collective-permute-done.5), channel_id=1, source_target_pairs={{0,4},{4,8},{8,12},{12,16},{16,20},{20,24},{24,28},{28,0},{1,5},{5... | collective-permute-start | bytes 12296 | tf_op jit(solution)/shard_map/ppermute | solution.py:16
  55.8 50.1 %copy-start.7 = (s32[1,1,192]{2,1,0:T(1,128)S(1)}, s32[1,1,192]{2,1,0:T(1,128)}, u32[]{:S(2)}) copy-start(s32[1,1,192]{2,1,0:T(1,128)} %param.10) | copy-start | bytes 2308
  61.9 51.8 %copy-start.9 = (u32[32]{0:T(128)S(1)}, u32[32]{0:T(128)}, u32[]{:S(2)}) copy-start(u32[32]{0:T(128)} %constant.70) | copy-start | bytes 388
  61.9 123.3 %copy-start.2 = (f32[1,16,128]{2,1,0:T(8,128)S(1)}, f32[1,16,128]{2,1,0:T(8,128)}, u32[]{:S(2)}) copy-start(f32[1,16,128]{2,1,0:T(8,128)} %param.8) | copy-start | bytes 24580
  69.1 0.6 copy-start.1
  69.8 114.6 %all-reduce.7.cloned.1.call-start = ((), (), s32[]{:S(2)}) async-start(), calls=%async_computation.1 | async-start | bytes 262144
  113.1 0.6 copy-start
  185.2 0.6 copy-start.3
Sparse Core Ops, SparseCore 0:
  69.9 29.2 all-reduce.4
  113.9 70.4 all-reduce.6
